TPU v7x, 32 devices: a whole 2x2x4 slice. The times are simulated.
32 devices in a mesh: dp: 16 (over z, y, core), tensor: 2 (over x).
Axes of the slice: x: 2, y: 2, z: 4, core: 2. Of those that a mesh axis runs over, the one named last changes fastest.
Arguments:
- tokens: bfloat16 [6144, 2880], P('dp', 'tensor'), may hold values from -6 to 6
- out_grad: bfloat16 [6144, 2880], P('dp', 'tensor'), may hold values from -6 to 6
- route_probs: bfloat16 [6144, 4], P('dp'), may hold values from 0.099609375 to 1
- expert_ids: int32 [6144, 4], P('dp'), may hold values from 0 to 63, all different within a row; in each aligned block of 384 rows (0 to 383, 384 to 767, ...) at most 36 rows name the same one
- placement_map: int32 [64], replicated, may hold values from 0 to 63, each once
- w_gate: bfloat16 [16, 2880, 2880], P('dp', None, 'tensor'), may hold values from -0.109375 to 0.109375
- w_up: bfloat16 [16, 2880, 2880], P('dp', None, 'tensor'), may hold values from -0.109375 to 0.109375
- w_down: bfloat16 [16, 2880, 2880], P('dp', 'tensor'), may hold values from -0.109375 to 0.109375
Outputs:
- input_grad: bfloat16 [6144, 2880], P('dp', 'tensor')
- gate_grad: bfloat16 [16, 2880, 2880], P('dp', None, 'tensor')
- up_grad: bfloat16 [16, 2880, 2880], P('dp', None, 'tensor')
- down_grad: bfloat16 [16, 2880, 2880], P('dp', 'tensor')
- prob_grad: bfloat16 [6144, 4], P('dp')
Inputs may be any that keep to these rules, and one draw needn't show every extreme that they name: `expert_ids`: each row names 4 different experts. In the rows of one index of dp no expert is named by more than 36 rows, a bound that some block reaches. `placement_map`: A permutation: every value is taken by exactly one expert.
All inputs are finite; a program needn't handle non-finite values.
Results may differ from a plain program's by a relative error of at most 0.011.
Values may be sent and summed in bfloat16 or wider, within the bound.
A program may use at most 128 MiB of HBM per device.

v0:
```python
import jax
import jax.numpy as jnp
from jax import lax
from jax.sharding import PartitionSpec as P

EXP_OWN = 4


SWISH_SLOPE = 1.702


def route_layout(expert_ids, placement_map, owners, capacity):
    tok_rows, top_count = expert_ids.shape
    experts = placement_map.shape[0]
    per_owner = experts // owners
    matches = expert_ids[:, :, None] == jnp.arange(experts, dtype=jnp.int32)[None, None, :]
    code_value = jnp.sum(jnp.where(matches, placement_map[None, None, :], 0), axis=-1).reshape(-1)
    in_wave = code_value % per_owner == 0
    owner_of = code_value // per_owner
    chosen = (
        (owner_of[:, None] == jnp.arange(owners, dtype=jnp.int32)[None, :]) & in_wave[:, None]
    ).astype(jnp.int32)
    before = jnp.cumsum(chosen, axis=0) - chosen
    slot_index = jnp.sum(before * chosen, axis=1)
    target = jnp.where(in_wave, owner_of * capacity + slot_index, owners * capacity)
    slot_route = (
        jnp.full((owners * capacity,), -1, jnp.int32)
        .at[target]
        .set(jnp.arange(tok_rows * top_count, dtype=jnp.int32), mode="drop")
    )
    return (in_wave, target, slot_route)


def build_rows(values, slot_route, row_valid, top_count):
    picked = jnp.take(values, jnp.where(row_valid, slot_route // top_count, 0), axis=0)
    return jnp.where(row_valid[:, None], picked, jnp.zeros_like(picked))


def shards(tokens, out_grad, route_probs, expert_ids, placement_map, w_gate, w_up, w_down):
    owners = lax.axis_size("dp")
    tok_rows, top_count = expert_ids.shape
    capacity = 3 * tok_rows * top_count // (2 * EXP_OWN * owners)
    in_wave, target, slot_route = route_layout(expert_ids, placement_map, owners, capacity)
    row_valid = slot_route >= 0
    safe_route = jnp.where(row_valid, slot_route, 0)
    zero_half = jnp.zeros((), jnp.bfloat16)
    prob_rows = jnp.where(row_valid, route_probs.reshape(-1)[safe_route], zero_half)
    part_width = tokens.shape[1]
    send_x = build_rows(tokens, slot_route, row_valid, top_count).reshape(
        owners, capacity, part_width
    )
    send_d = build_rows(out_grad, slot_route, row_valid, top_count).reshape(
        owners, capacity, part_width
    )
    got_x, got_d, got_p = (
        lax.all_to_all(send_x, "dp", split_axis=0, concat_axis=0, tiled=True),
        lax.all_to_all(send_d, "dp", split_axis=0, concat_axis=0, tiled=True),
        lax.all_to_all(
            prob_rows.reshape(owners, capacity), "dp", split_axis=0, concat_axis=0, tiled=True
        ),
    )
    rows_x, rows_d = (
        lax.all_gather(got_x.reshape(owners * capacity, part_width), "tensor", axis=1, tiled=True),
        lax.all_gather(got_d.reshape(owners * capacity, part_width), "tensor", axis=1, tiled=True),
    )
    prob_column = got_p.reshape(-1).astype(jnp.float32)[:, None]
    gate_w = w_gate[0]
    up_w = w_up[0]
    down_w = w_down[0]
    contract_cols = (((1,), (1,)), ((), ()))
    contract_rows = (((0,), (0,)), ((), ()))
    gate_pre = jnp.dot(rows_x, gate_w, preferred_element_type=jnp.float32)
    up_pre = jnp.dot(rows_x, up_w, preferred_element_type=jnp.float32)
    sig_gate = jax.nn.sigmoid(SWISH_SLOPE * gate_pre)
    active = (gate_pre * sig_gate * (up_pre + 1.0)).astype(jnp.bfloat16)
    down_back = lax.dot_general(rows_d, down_w, contract_cols, preferred_element_type=jnp.float32)
    outputs = jnp.dot(active, down_w, preferred_element_type=jnp.float32)
    slice_sum = jnp.sum(rows_d.astype(jnp.float32) * outputs, axis=1)
    prob_sum = lax.psum(slice_sum, "tensor")
    delta_act = prob_column * down_back
    grad_gate_pre = (
        delta_act
        * (up_pre + 1.0)
        * (sig_gate + SWISH_SLOPE * gate_pre * sig_gate * (1.0 - sig_gate))
    ).astype(jnp.bfloat16)
    grad_up_pre = (delta_act * gate_pre * sig_gate).astype(jnp.bfloat16)
    scaled_grad = (prob_column * rows_d.astype(jnp.float32)).astype(jnp.bfloat16)
    down_grad = lax.dot_general(
        active, scaled_grad, contract_rows, preferred_element_type=jnp.float32
    ).astype(jnp.bfloat16)
    gate_grad = lax.dot_general(
        rows_x, grad_gate_pre, contract_rows, preferred_element_type=jnp.float32
    ).astype(jnp.bfloat16)
    up_grad = lax.dot_general(
        rows_x, grad_up_pre, contract_rows, preferred_element_type=jnp.float32
    ).astype(jnp.bfloat16)
    input_part = lax.dot_general(
        grad_gate_pre, gate_w, contract_cols, preferred_element_type=jnp.float32
    ) + lax.dot_general(grad_up_pre, up_w, contract_cols, preferred_element_type=jnp.float32)
    rounded_part = lax.optimization_barrier(input_part.astype(jnp.bfloat16)).astype(jnp.float32)
    input_rows = lax.psum_scatter(
        rounded_part.astype(jnp.bfloat16), "tensor", scatter_dimension=1, tiled=True
    )
    part_cols = input_rows.shape[1]
    back_rows, back_prob = (
        lax.all_to_all(
            input_rows.reshape(owners, capacity, part_cols),
            "dp",
            split_axis=0,
            concat_axis=0,
            tiled=True,
        ),
        lax.all_to_all(
            prob_sum.astype(jnp.bfloat16).reshape(owners, capacity),
            "dp",
            split_axis=0,
            concat_axis=0,
            tiled=True,
        ),
    )
    back_rows = back_rows.reshape(owners * capacity, part_cols)
    back_prob = back_prob.reshape(-1)
    safe_target = jnp.where(in_wave, target, 0)
    route_rows = jnp.where(in_wave[:, None], jnp.take(back_rows, safe_target, axis=0), zero_half)
    input_grad = jnp.sum(
        route_rows.reshape(tok_rows, top_count, part_cols).astype(jnp.float32), axis=1
    ).astype(jnp.bfloat16)
    prob_grad = jnp.where(in_wave, back_prob[safe_target], zero_half).reshape(tok_rows, top_count)
    return (input_grad, gate_grad[None], up_grad[None], down_grad[None], prob_grad)


def solution(mesh):
    in_specs = (
        P("dp", "tensor"),
        P("dp", "tensor"),
        P("dp", None),
        P("dp", None),
        P(),
        P("dp", None, "tensor"),
        P("dp", None, "tensor"),
        P("dp", "tensor", None),
    )
    out_specs = (
        P("dp", "tensor"),
        P("dp", None, "tensor"),
        P("dp", None, "tensor"),
        P("dp", "tensor", None),
        P("dp", None),
    )
    return jax.shard_map(shards, mesh=mesh, in_specs=in_specs, out_specs=out_specs, check_vma=False)
```

profile of v0, /device:TPU:13, one launch (start us, length us, event | category | flops | bytes accessed | tf_op | source)
XLA Modules:
  0.0 413.7 jit_solution(8770292031321615427)
XLA Ops:
  7.2 0.9 select_reduce_fusion.1
  8.8 4.5 %reduce-window.6 = s32[16,12,128]{2,1,0:T(8,128)S(1)} reduce-window(s32[16,12,128]{2,1,0:T(8,128)S(1)} %fusion.30, s32[]{:T(128)} %constant.77.clone.1), window={size=1x1x128 pad=0_0x0_0x127_0}, to_apply=%region_1.2 | reduce-window | flops 3121152 | bytes 196612 | tf_op jit(solution)/shard_map/reduce-window
  14.2 0.7 fusion.40
  14.8 6.2 %scatter_custom_fusion = s32[576]{0:T(1024)S(1)} fusion(s32[1536]{0:T(1024)S(1)} %get-tuple-element.22, s32[1536]{0:T(1024)S(1)} %iota.15, s32[]{:T(128)} %constant.82.clone.1), kind=kCustom, calls=%fused_computation.111 | custom fusion | bytes 2308 | tf_op jit(solution)/shard_map/scatter | solution.py:29
  21.1 1.6 copy.45
  22.7 1.2 copy.43
  23.9 3.6 gather_fusion.4
  27.5 3.6 gather_fusion.3
  31.1 3.8 select_select_fusion
  34.8 2.6 reshape.291
  37.5 50.9 %all_to_all.35 = bf16[16,36,1440]{2,1,0:T(8,128)(2,1)} all-to-all(bf16[16,36,1440]{2,1,0:T(8,128)(2,1)S(1)} %reshape.291), channel_id=1, replica_groups=mesh['dp'=16,'tensor'=2] {'dp'}, dimensions={0} | all-to-all | bytes 3317760 | tf_op jit(solution)/shard_map/all_to_all | solution.py:56
  88.4 3.8 reshape.292
  92.2 2.6 reshape.289
  94.9 49.4 %all_to_all.36 = bf16[16,36,1440]{2,1,0:T(8,128)(2,1)} all-to-all(bf16[16,36,1440]{2,1,0:T(8,128)(2,1)S(1)} %reshape.289), channel_id=1, replica_groups=mesh['dp'=16,'tensor'=2] {'dp'}, dimensions={0} | all-to-all | bytes 3317760 | tf_op jit(solution)/shard_map/all_to_all | solution.py:57
  144.2 3.8 reshape.290
  148.5 3.9 gather_fusion
  152.6 9.0 %all_to_all.37 = bf16[16,1,36]{2,1,0:T(2,128)(2,1)S(1)} all-to-all(bf16[16,1,36]{2,1,0:T(2,128)(2,1)S(1)} %all_to_all.28), channel_id=1, replica_groups=mesh['dp'=16,'tensor'=2] {'dp'}, dimensions={0} | all-to-all | bytes 2304 | tf_op jit(solution)/shard_map/all_to_all | solution.py:58
  161.6 0.7 reshape.296
  162.3 5.6 %copy.46 = bf16[2,1440,576]{1,0,2:T(2,128)(2,1)S(1)} copy(bf16[2,1440,576]{1,2,0:T(8,128)(2,1)} %all-gather.7.cloned.1.call-done) | data formatting | bytes 6635520 | tf_op jit(solution)/shard_map/all_gather | solution.py:63
  167.9 4.1 %reshape.351 = bf16[2880,576]{0,1:T(8,128)(2,1)} reshape(bf16[2,1440,576]{1,0,2:T(2,128)(2,1)S(1)} %copy.46) | data formatting | bytes 6635520
  172.0 25.0 %all-gather.5.cloned.1.call-done = bf16[2,1440,576]{1,2,0:T(8,128)(2,1)} async-done(((bf16[1,1440,576]{1,2,0:T(8,128)(2,1)}), bf16[2,1440,576]{1,2,0:T(8,128)(2,1)}) %all-gather.5.cloned.1.call-update) | async-done | bytes 3317776 | tf_op jit(solution)/shard_map/all_gather | solution.py:64
  197.0 5.6 %copy.44 = bf16[2,1440,576]{1,0,2:T(2,128)(2,1)S(1)} copy(bf16[2,1440,576]{1,2,0:T(8,128)(2,1)} %all-gather.5.cloned.1.call-done) | data formatting | bytes 6635520 | tf_op jit(solution)/shard_map/all_gather | solution.py:64
  202.7 4.2 %reshape.349 = bf16[2880,576]{0,1:T(8,128)(2,1)} reshape(bf16[2,1440,576]{1,0,2:T(2,128)(2,1)S(1)} %copy.44) | data formatting | bytes 6635520
  206.8 11.2 %fusion.5 = f32[576,1440]{1,0:T(8,128)} fusion(bf16[2880,576]{0,1:T(8,128)(2,1)} %reshape.351, bf16[1,2880,1440]{1,2,0:T(8,128)(2,1)} %param.15), kind=kOutput, calls=%fused_computation.14 | convolution fusion | flops 4777574400 | bytes 14929920 | tf_op jit(solution)/shard_map/dot_general | solution.py:72
  218.0 19.8 %fusion.21 = f32[576,1440]{1,0:T(8,128)S(1)} fusion(bf16[2880,576]{0,1:T(8,128)(2,1)S(1)} %copy-done.4, bf16[1,1440,2880]{2,1,0:T(8,128)(2,1)} %param.17, f32[576]{0:T(1024)S(1)} %copy-done.8), kind=kOutput, calls=%fused_computation.30 | convolution fusion | flops 4778403840 | bytes 14932224 | tf_op jit(solution)/shard_map/dot_general | solution.py:76
  237.9 12.5 %multiply_convert_fusion = (bf16[576,1440]{1,0:T(8,128)(2,1)}, bf16[576,1440]{1,0:T(8,128)(2,1)}, bf16[576,1440]{1,0:T(8,128)(2,1)S(1)}) fusion(f32[576,1440]{1,0:T(8,128)} %fusion.5, f32[576,1440]{1,0:T(8,128)S(1)} %fusion.21, bf16[2880,576]{0,1:T(8,128)(2,1)S(1)} %copy-done.1, bf16[1,2880,1440]{1,2,0:T(8,128)(2,1)} %param.16), kind=kOutput, calls=%fused_computation.31 | convolution fusion | flops 4792504320 | bytes 23224320 | tf_op jit(solution)/shard_map/dot_general | solution.py:73
  250.3 9.3 %fusion.3 = f32[576,2880]{1,0:T(8,128)S(1)} fusion(bf16[576,1440]{1,0:T(8,128)(2,1)} %get-tuple-element.30, bf16[1,2880,1440]{1,2,0:T(8,128)(2,1)} %param.15), kind=kOutput, calls=%fused_computation.12 | convolution fusion | flops 4777574400 | bytes 16588800 | tf_op jit(solution)/shard_map/dot_general | solution.py:97
  259.7 9.5 %add_convert_fusion = bf16[576,2880]{1,0:T(8,128)(2,1)S(1)} fusion(f32[576,2880]{1,0:T(8,128)S(1)} %fusion.3, bf16[576,1440]{1,0:T(8,128)(2,1)S(1)} %get-tuple-element.31, bf16[1,2880,1440]{1,2,0:T(8,128)(2,1)} %param.16), kind=kOutput, calls=%fused_computation.28 | convolution fusion | flops 4780892160 | bytes 19906560 | tf_op jit(solution)/shard_map/dot_general | solution.py:99
  269.2 3.7 copy.50
  273.6 9.5 %fusion.16 = f32[576]{0:T(1024)S(1)} fusion(bf16[2880,576]{0,1:T(8,128)(2,1)} %reshape.349, bf16[576,1440]{1,0:T(8,128)(2,1)} %get-tuple-element.29, bf16[1,1440,2880]{2,1,0:T(8,128)(2,1)} %param.17), kind=kOutput, calls=%fused_computation.27 | convolution fusion | flops 4782550528 | bytes 13273344 | tf_op jit(solution)/shard_map/dot_general | solution.py:77
  283.2 4.4 %psum.7 = bf16[576]{0:T(1024)(128)(2,1)S(1)} all-reduce(f32[576]{0:T(1024)S(1)} %fusion.16), channel_id=1, replica_groups=mesh['dp'=16,'tensor'=2] {'tensor'}, use_global_device_ids=true, to_apply=%region_8.10 | all-reduce | flops 576 | bytes 3456 | tf_op jit(solution)/shard_map/psum | solution.py:79
  287.5 0.7 all_to_all.29
  288.2 7.3 %all-to-all-start.4 = ((bf16[16,1,36]{2,1,0:T(2,128)(2,1)}), bf16[16,1,36]{2,1,0:T(2,128)(2,1)S(1)}, u32[]{:S(2)}, u32[]{:S(2)}) async-start(bf16[16,1,36]{2,1,0:T(2,128)(2,1)} %all_to_all.29), calls=%async_computation.4 | async-start | bytes 16384 | tf_op jit(solution)/shard_map/all_to_all | solution.py:113
  295.5 10.8 %fusion.2 = bf16[1,2880,1440]{1,2,0:T(8,128)(2,1)} fusion(bf16[2880,576]{0,1:T(8,128)(2,1)S(1)} %copy-done.2, bf16[576,1440]{1,0:T(8,128)(2,1)} %copy-done.10), kind=kOutput, calls=%fused_computation.11 | convolution fusion | flops 4781721600 | bytes 13271040 | tf_op jit(solution)/shard_map/dot_general | solution.py:94
  306.3 16.3 %reduce-scatter.4.cloned.1.call-done = bf16[1440,576]{1,0:T(8,128)(2,1)} async-done(((bf16[2880,576]{1,0:T(8,128)(2,1)}), bf16[1440,576]{1,0:T(8,128)(2,1)}) %reduce-scatter.4.cloned.1.call-update) | async-done | bytes 1658896
  322.6 2.6 copy.51
  325.2 1.6 reshape.293
  326.8 7.1 %all-to-all-start.3 = ((bf16[16,36,1440]{2,1,0:T(8,128)(2,1)}), bf16[16,36,1440]{2,1,0:T(8,128)(2,1)}, u32[]{:S(2)}, u32[]{:S(2)}) async-start(bf16[16,36,1440]{2,1,0:T(8,128)(2,1)} %reshape.293), calls=%async_computation.3 | async-start | bytes 3932160 | tf_op jit(solution)/shard_map/all_to_all | solution.py:106
  333.9 10.9 %fusion.1 = bf16[1,2880,1440]{1,2,0:T(8,128)(2,1)} fusion(bf16[2880,576]{0,1:T(8,128)(2,1)S(1)} %copy-done.3, bf16[576,1440]{1,0:T(8,128)(2,1)} %get-tuple-element.30), kind=kOutput, calls=%fused_computation.10 | convolution fusion | flops 4781721600 | bytes 13271040 | tf_op jit(solution)/shard_map/dot_general | solution.py:91
  344.9 9.5 %fusion = bf16[1,1440,2880]{2,1,0:T(8,128)(2,1)} fusion(bf16[576,1440]{1,0:T(8,128)(2,1)S(1)} %copy-done.11, bf16[2880,576]{0,1:T(8,128)(2,1)S(1)} %copy-done.5, f32[576]{0:T(1024)S(1)} %copy-done.8), kind=kOutput, calls=%fused_computation.9 | convolution fusion | flops 4786698240 | bytes 13273344 | tf_op jit(solution)/shard_map/dot_general | solution.py:88
  354.5 9.5 %gather_fusion.2 = bf16[1536]{0:T(1024)(128)(2,1)S(1)} fusion(bf16[576]{0:T(1024)(128)(2,1)S(1)} %reshape.295, s32[2048]{0:T(1024)S(1)} %pad_clamp_fusion), kind=kCustom, calls=%fused_computation.4 | custom fusion | bytes 12288 | tf_op jit(solution)/shard_map/gather | solution.py:128
  364.3 0.6 broadcast_select_fusion
  365.3 13.1 %all-to-all-done.3 = bf16[16,36,1440]{2,1,0:T(8,128)(2,1)} async-done(((bf16[16,36,1440]{2,1,0:T(8,128)(2,1)}), bf16[16,36,1440]{2,1,0:T(8,128)(2,1)}, u32[]{:S(2)}, u32[]{:S(2)}) %all-to-all-start.3) | async-done | bytes 1658912 | tf_op jit(solution)/shard_map/all_to_all | solution.py:106
  378.5 2.7 reshape.294
  381.2 6.2 %gather_fusion.1 = bf16[1536,1440]{1,0:T(8,128)(2,1)} fusion(bf16[576,1440]{1,0:T(8,128)(2,1)S(1)} %reshape.294, s32[2048]{0:T(1024)S(1)} %pad_clamp_fusion), kind=kCustom, calls=%fused_computation.3 | custom fusion | bytes 8853504 | tf_op jit(solution)/shard_map/jit(_take)/gather | solution.py:124
  387.4 8.9 %gather.19 = bf16[384,4,1440]{2,1,0:T(4,128)(2,1)} reshape(bf16[1536,1440]{1,0:T(8,128)(2,1)} %gather_fusion.1) | data formatting | bytes 8847360 | tf_op jit(solution)/shard_map/jit(_take)/gather | solution.py:124
  396.3 9.1 %select_reduce_fusion = bf16[384,1440]{1,0:T(8,128)(2,1)S(1)} fusion(bf16[384,4,1440]{2,1,0:T(4,128)(2,1)} %gather.19, pred[384,4]{1,0:T(8,128)(4,1)S(1)} %copy.39, pred[384,4]{1,0:T(8,128)(4,1)S(1)} %copy.35), kind=kLoop, calls=%fused_computation.29 | loop fusion | flops 6082560 | bytes 5532672 | tf_op jit(solution)/shard_map/reduce_sum | solution.py:125
  405.4 1.4 copy.49
  (65 shorter events, 3.6 us)
Async XLA Ops:
  7.2 15.5 %copy-start.6 = (bf16[384,1440]{0,1:T(8,128)(2,1)S(1)}, bf16[384,1440]{0,1:T(8,128)(2,1)}, u32[]{:S(2)}) copy-start(bf16[384,1440]{0,1:T(8,128)(2,1)} %param.11) | copy-start | bytes 3317764
  7.2 155.1 %all-gather.7.cloned.1.call-start = ((), (), s32[]{:S(2)}) async-start(), calls=%async_computation.7 | async-start | bytes 5308416 | tf_op jit(solution)/shard_map/all_gather | solution.py:63
  27.5 3.6 copy-start
  92.2 104.8 %all-gather.5.cloned.1.call-start = ((), (), s32[]{:S(2)}) async-start(), calls=%async_computation.6 | async-start | bytes 5308416 | tf_op jit(solution)/shard_map/all_gather | solution.py:64
  144.2 3.9 copy-start.9
  148.1 174.5 %reduce-scatter.4.cloned.1.call-start = ((), (), s32[]{:S(2)}) async-start(), calls=%async_computation.8 | async-start | bytes 5529600
  206.8 11.2 %copy-start.4 = (bf16[2880,576]{0,1:T(8,128)(2,1)S(1)}, bf16[2880,576]{0,1:T(8,128)(2,1)}, u32[]{:S(2)}) copy-start(bf16[2880,576]{0,1:T(8,128)(2,1)} %reshape.349) | copy-start | bytes 9953284
  206.8 11.2 %copy-start.8 = (f32[576]{0:T(1024)S(1)}, f32[576]{0:T(1024)}, u32[]{:S(2)}) copy-start(f32[576]{0:T(1024)} %reshape.296) | copy-start | bytes 6916
  218.0 19.8 %copy-start.1 = (bf16[2880,576]{0,1:T(8,128)(2,1)S(1)}, bf16[2880,576]{0,1:T(8,128)(2,1)}, u32[]{:S(2)}) copy-start(bf16[2880,576]{0,1:T(8,128)(2,1)} %reshape.351) | copy-start | bytes 9953284
  250.3 9.3 %copy-start.10 = (bf16[576,1440]{1,0:T(8,128)(2,1)}, bf16[576,1440]{1,0:T(8,128)(2,1)S(1)}, u32[]{:S(2)}) copy-start(bf16[576,1440]{1,0:T(8,128)(2,1)S(1)} %get-tuple-element.31) | copy-start | bytes 4976644
  272.9 0.7 copy-start.7
  273.6 21.9 %copy-start.2 = (bf16[2880,576]{0,1:T(8,128)(2,1)S(1)}, bf16[2880,576]{0,1:T(8,128)(2,1)}, u32[]{:S(2)}) copy-start(bf16[2880,576]{0,1:T(8,128)(2,1)} %reshape.351) | copy-start | bytes 9953284
  288.2 38.5 %all-to-all-start.4 = ((bf16[16,1,36]{2,1,0:T(2,128)(2,1)}), bf16[16,1,36]{2,1,0:T(2,128)(2,1)S(1)}, u32[]{:S(2)}, u32[]{:S(2)}) async-start(bf16[16,1,36]{2,1,0:T(2,128)(2,1)} %all_to_all.29), calls=%async_computation.4 | async-start | bytes 16384 | tf_op jit(solution)/shard_map/all_to_all | solution.py:113
  326.8 7.1 %copy-start.3 = (bf16[2880,576]{0,1:T(8,128)(2,1)S(1)}, bf16[2880,576]{0,1:T(8,128)(2,1)}, u32[]{:S(2)}) copy-start(bf16[2880,576]{0,1:T(8,128)(2,1)} %reshape.351) | copy-start | bytes 9953284
  326.8 51.7 %all-to-all-start.3 = ((bf16[16,36,1440]{2,1,0:T(8,128)(2,1)}), bf16[16,36,1440]{2,1,0:T(8,128)(2,1)}, u32[]{:S(2)}, u32[]{:S(2)}) async-start(bf16[16,36,1440]{2,1,0:T(8,128)(2,1)} %reshape.293), calls=%async_computation.3 | async-start | bytes 3932160 | tf_op jit(solution)/shard_map/all_to_all | solution.py:106
  333.9 11.0 %copy-start.5 = (bf16[2880,576]{0,1:T(8,128)(2,1)S(1)}, bf16[2880,576]{0,1:T(8,128)(2,1)}, u32[]{:S(2)}) copy-start(bf16[2880,576]{0,1:T(8,128)(2,1)} %reshape.349) | copy-start | bytes 9953284
  333.9 11.0 %copy-start.11 = (bf16[576,1440]{1,0:T(8,128)(2,1)S(1)}, bf16[576,1440]{1,0:T(8,128)(2,1)}, u32[]{:S(2)}) copy-start(bf16[576,1440]{1,0:T(8,128)(2,1)} %get-tuple-element.29) | copy-start | bytes 4976644
Sparse Core Ops, SparseCore 0:
  92.3 48.7 all-gather.6
  148.2 48.7 all-gather.4
  273.1 49.4 reduce-scatter.3
where the time goes:
time: 421 us; the launch traced here: 414 us
  blocking collectives  114 us (27%)
  matrix products  103 us (24%)
  local copies, waits for them, and re-layouts  93.4 us (22%)
  waiting for transfers between devices  54.4 us (13%)
  other arithmetic  20.1 us (5%)
  starting transfers between devices  14.5 us (3%)
  between operations  14.5 us (3%)
    all_to_all x1, blocking collectives, shards(): lax.all_to_all(send_x, 'dp', split_axis=0, concat_axis=0, tiled=True)  50.9 us
    all_to_all x1, blocking collectives, shards(): lax.all_to_all(send_d, 'dp', split_axis=0, concat_axis=0, tiled=True)  49.4 us
    all_gather x1, waiting for transfers between devices, shards(): lax.all_gather(got_d.reshape(owners * capacity, part_width), 'tensor', ax...  25 us
    dot_general x1, matrix products, shards(): lax.dot_general(rows_d, down_w, contract_cols, preferred_element_type=jnp...  19.8 us
    unnamed x32, local copies, waits for them, and re-layouts  19.4 us
    unnamed x4, waiting for transfers between devices  16.3 us
    gather x2, local copies, waits for them, and re-layouts, shards(): jnp.take(back_rows, safe_target, axis=0)  15.2 us
    all_to_all x1, waiting for transfers between devices, shards(): lax.all_to_all(input_rows.reshape(owners, capacity, part_cols), 'dp', spl...  13.1 us
  transfers between devices with their start and end apart: 5, of which 3 were waited for; matrix products, arithmetic and copies ran while one was open for 19% of the time, Pallas kernels for 0%

commit v1 on v0

v1 whole, which is shorter than its diff:
```python
import jax
import jax.numpy as jnp
from jax import lax
from jax.sharding import PartitionSpec as P

EXP_OWN = 4


SWISH_SLOPE = 1.702


def swap(values):
    count = lax.axis_size("tensor")
    return lax.ppermute(values, "tensor", [(i, (i + 1) % count) for i in range(count)])


def join(mine, other, width):
    first = lax.axis_index("tensor") == 0
    low = jnp.where(first, mine, other)[:, :width]
    high = jnp.where(first, other, mine)[:, :width]
    return jnp.concatenate([low, high], axis=1)


def gather_columns(mine, width):
    if lax.axis_size("tensor") == 2:
        return join(mine, swap(mine), width)
    return lax.all_gather(mine[:, :width], "tensor", axis=1, tiled=True)


def scatter_columns(part, width):
    if lax.axis_size("tensor") != 2:
        return lax.psum_scatter(part, "tensor", scatter_dimension=1, tiled=True)
    first = lax.axis_index("tensor") == 0
    low, high = part[:, :width], part[:, width:]
    other = swap(jnp.where(first, high, low)).astype(jnp.float32)
    return (jnp.where(first, low, high).astype(jnp.float32) + other).astype(jnp.bfloat16)


def total(values):
    if lax.axis_size("tensor") == 2:
        return values + swap(values)
    return lax.psum(values, "tensor")


def shards(tokens, out_grad, route_probs, expert_ids, placement_map, w_gate, w_up, w_down):
    owners = lax.axis_size("dp")
    tok_rows, top_count = expert_ids.shape
    experts = placement_map.shape[0]
    per_owner = experts // owners
    capacity = 3 * tok_rows * top_count // (2 * EXP_OWN * owners)
    slots = capacity
    rows = owners * slots
    width = tokens.shape[1]
    half = jnp.bfloat16

    matches = expert_ids[:, :, None] == jnp.arange(experts, dtype=jnp.int32)[None, None, :]
    code_value = jnp.sum(jnp.where(matches, placement_map[None, None, :], 0), axis=-1)
    wave_codes = per_owner * jnp.arange(owners, dtype=jnp.int32)
    pick = code_value[:, :, None] == wave_codes[None, None, :]
    member = jnp.sum(pick.astype(jnp.float32), axis=1)
    probs_to = jnp.sum(
        jnp.where(pick, route_probs[:, :, None].astype(jnp.float32), 0.0), axis=1
    ).astype(half)
    earlier = (
        jnp.arange(tok_rows)[None, :] < jnp.arange(tok_rows)[:, None]
    ).astype(half)
    slot = lax.dot_general(
        member.astype(half), earlier, (((0,), (1,)), ((), ())), preferred_element_type=jnp.float32
    )
    key = jnp.where(member.T > 0, slot, -1.0).astype(jnp.int32)
    placed = key[:, None, :] == jnp.arange(slots, dtype=jnp.int32)[None, :, None]
    onehot = placed.astype(half).reshape(rows, tok_rows)

    def exchange(values):
        out = lax.all_to_all(
            values.reshape(owners, slots, values.shape[1]),
            "dp",
            split_axis=0,
            concat_axis=0,
            tiled=True,
        )
        return out.reshape(rows, values.shape[1])

    grad_and_prob = jnp.concatenate([out_grad, probs_to], axis=1)
    got_x = exchange(jnp.dot(onehot, tokens, preferred_element_type=jnp.float32).astype(half))
    send_d = jnp.dot(onehot, grad_and_prob, preferred_element_type=jnp.float32).astype(half)
    got_d = exchange(send_d)
    rows_x = gather_columns(got_x, width)
    rows_d = gather_columns(got_d, width)
    mine = jnp.arange(owners) == lax.axis_index("dp")
    prob_column = jnp.sum(
        jnp.where(mine[None, :], got_d[:, width:].astype(jnp.float32), 0.0), axis=1, keepdims=True
    )

    gate_w = w_gate[0]
    up_w = w_up[0]
    down_w = w_down[0]
    contract_cols = (((1,), (1,)), ((), ()))
    contract_rows = (((0,), (0,)), ((), ()))
    gate_pre = jnp.dot(rows_x, gate_w, preferred_element_type=jnp.float32)
    up_pre = jnp.dot(rows_x, up_w, preferred_element_type=jnp.float32)
    sig_gate = jax.nn.sigmoid(SWISH_SLOPE * gate_pre)
    active = (gate_pre * sig_gate * (up_pre + 1.0)).astype(half)
    down_back = lax.dot_general(rows_d, down_w, contract_cols, preferred_element_type=jnp.float32)
    slice_sum = jnp.sum(active.astype(jnp.float32) * down_back, axis=1)
    prob_sum = total(slice_sum)
    delta_act = prob_column * down_back
    grad_gate_pre = (
        delta_act
        * (up_pre + 1.0)
        * (sig_gate + SWISH_SLOPE * gate_pre * sig_gate * (1.0 - sig_gate))
    ).astype(half)
    grad_up_pre = (delta_act * gate_pre * sig_gate).astype(half)
    scaled_grad = (prob_column * rows_d.astype(jnp.float32)).astype(half)
    input_part = lax.dot_general(
        grad_gate_pre, gate_w, contract_cols, preferred_element_type=jnp.float32
    ) + lax.dot_general(grad_up_pre, up_w, contract_cols, preferred_element_type=jnp.float32)
    rounded_part = lax.optimization_barrier(input_part.astype(half))
    input_rows = scatter_columns(rounded_part, width)
    back = exchange(jnp.concatenate([input_rows, prob_sum.astype(half)[:, None]], axis=1))

    down_grad = lax.dot_general(
        active, scaled_grad, contract_rows, preferred_element_type=jnp.float32
    ).astype(half)
    gate_grad = lax.dot_general(
        rows_x, grad_gate_pre, contract_rows, preferred_element_type=jnp.float32
    ).astype(half)
    up_grad = lax.dot_general(
        rows_x, grad_up_pre, contract_rows, preferred_element_type=jnp.float32
    ).astype(half)

    combined = lax.dot_general(onehot, back, contract_rows, preferred_element_type=jnp.float32)
    input_grad = combined[:, :width].astype(half)
    back_prob = back[:, width].astype(jnp.float32).reshape(owners, slots)
    prob_to = jnp.sum(jnp.where(placed, back_prob[:, :, None], 0.0), axis=1).T
    prob_grad = jnp.sum(jnp.where(pick, prob_to[:, None, :], 0.0), axis=2).astype(half)
    return (input_grad, gate_grad[None], up_grad[None], down_grad[None], prob_grad)


def solution(mesh):
    in_specs = (
        P("dp", "tensor"),
        P("dp", "tensor"),
        P("dp", None),
        P("dp", None),
        P(),
        P("dp", None, "tensor"),
        P("dp", None, "tensor"),
        P("dp", "tensor", None),
    )
    out_specs = (
        P("dp", "tensor"),
        P("dp", None, "tensor"),
        P("dp", None, "tensor"),
        P("dp", "tensor", None),
        P("dp", None),
    )
    return jax.shard_map(shards, mesh=mesh, in_specs=in_specs, out_specs=out_specs, check_vma=False)
```

time: 421 us -> 295 us (0.70)
  blocking collectives: 114 us -> 0 us
  waiting for transfers between devices: 54.4 us -> 149 us
  local copies, waits for them, and re-layouts: 93.4 us -> 16.4 us
  matrix products: 103 us -> 87 us
  between operations: 14.5 us -> 1.32 us
  starting transfers between devices: 14.5 us -> 21.7 us
  other arithmetic: 20.1 us -> 15.6 us
    all_to_all x3 -> x0, blocking collectives: 109 us -> none  [the longest x1 50.9 us: shards(): lax.all_to_all(send_x, 'dp', split_axis=0, concat_axis=0, tiled=True)]
    all_to_all x2 -> x3, waiting for transfers between devices: 13.1 us -> 93.7 us  [exchange(): lax.all_to_all(values.reshape(owners, slots, values.shape[1]), 'dp', spli...]
    ppermute x0 -> x4, waiting for transfers between devices: none -> 55 us  [swap(): lax.ppermute(values, 'tensor', [(i, (i + 1) % count) for i in range(count)])]
    gather x8 -> x0, local copies, waits for them, and re-layouts: 36.1 us -> none  [the longest x2 15.2 us: shards(): jnp.take(back_rows, safe_target, axis=0)]
    all_gather x2 -> x0, waiting for transfers between devices: 25 us -> none  [the longest x1 25 us: shards(): lax.all_gather(got_d.reshape(owners * capacity, part_width), 'tensor', ax...]
    unnamed x32 -> x44, local copies, waits for them, and re-layouts: 19.4 us -> 1.19 us
    unnamed x4 -> x0, waiting for transfers between devices: 16.3 us -> none
    all_gather x2 -> x0, local copies, waits for them, and re-layouts: 11.3 us -> none  [the longest x1 5.64 us: shards(): lax.all_gather(got_x.reshape(owners * capacity, part_width), 'tensor', ax...]
  transfers between devices with their start and end apart: 5 -> 7, of which waited for: 3 -> 5; matrix products, arithmetic and copies ran while one was open for 19% -> 22% of each run, Pallas kernels for 0% -> 0%
where the time goes in v1:
time: 295 us; the launch traced here: 291 us
  waiting for transfers between devices  149 us (51%)
  matrix products  87 us (29%)
  starting transfers between devices  21.7 us (7%)
  local copies, waits for them, and re-layouts  16.4 us (6%)
  other arithmetic  15.6 us (5%)
    all_to_all x3, waiting for transfers between devices, exchange(): lax.all_to_all(values.reshape(owners, slots, values.shape[1]), 'dp', spli...  93.7 us
    ppermute x4, waiting for transfers between devices, swap(): lax.ppermute(values, 'tensor', [(i, (i + 1) % count) for i in range(count)])  55 us
    all_to_all x3, starting transfers between devices, exchange(): lax.all_to_all(values.reshape(owners, slots, values.shape[1]), 'dp', spli...  17.8 us
    dot_general x1, matrix products, shards(): lax.dot_general(rows_d, down_w, contract_cols, preferred_element_type=jnp...  12.6 us
    dot_general x1, matrix products, shards(): lax.dot_general(active, scaled_grad, contract_rows, preferred_element_typ...  12.6 us
    dot_general x1, matrix products, shards(): lax.dot_general(rows_x, grad_gate_pre, contract_rows, preferred_element_t...  10.1 us
    dot_general x1, matrix products, shards(): lax.dot_general(rows_x, grad_up_pre, contract_rows, preferred_element_typ...  9.88 us
    dot_general x1, matrix products, shards(): up_pre = jnp.dot(rows_x, up_w, preferred_element_type=jnp.float32)  9.62 us
  transfers between devices with their start and end apart: 7, of which 5 were waited for; matrix products, arithmetic and copies ran while one was open for 22% of the time, Pallas kernels for 0%

profile of v1, /device:TPU:13, one launch (start us, length us, event | category | flops | bytes accessed | tf_op | source)
XLA Modules:
  0.0 290.7 jit_solution(6524013223070220815)
XLA Ops:
  0.7 0.8 convert_element_type.86
  1.5 0.8 select_reduce_fusion.1
  2.5 0.5 copy-done.11
  3.0 0.1 fusion.22
  3.2 0.6 copy-done.9
  3.8 0.1 eq.77
  3.9 0.2 broadcast_compare_fusion
  4.1 1.1 convolution_convert_fusion.3
  5.3 1.5 reshape.57
  6.8 6.7 %all-to-all-start.1 = ((bf16[16,36,1440]{2,1,0:T(8,128)(2,1)}), bf16[16,36,1440]{2,1,0:T(8,128)(2,1)}, u32[]{:S(2)}, u32[]{:S(2)}) async-start(bf16[16,36,1440]{2,1,0:T(8,128)(2,1)} %reshape.57), calls=%async_computation.1 | async-start | bytes 3932160 | tf_op jit(solution)/shard_map/all_to_all | solution.py:75
  13.5 1.1 convolution_convert_fusion.4
  14.6 1.5 reshape.55
  16.1 42.1 %all-to-all-done.1 = bf16[16,36,1440]{2,1,0:T(8,128)(2,1)} async-done(((bf16[16,36,1440]{2,1,0:T(8,128)(2,1)}), bf16[16,36,1440]{2,1,0:T(8,128)(2,1)}, u32[]{:S(2)}, u32[]{:S(2)}) %all-to-all-start.1) | async-done | bytes 1658912 | tf_op jit(solution)/shard_map/all_to_all | solution.py:75
  58.2 5.2 %all-to-all-start = ((bf16[16,36,1456]{2,1,0:T(8,128)(2,1)}), bf16[16,36,1456]{2,1,0:T(8,128)(2,1)S(1)}, u32[]{:S(2)}, u32[]{:S(2)}) async-start(bf16[16,36,1456]{2,1,0:T(8,128)(2,1)} %reshape.55), calls=%async_computation | async-start | bytes 3932160 | tf_op jit(solution)/shard_map/all_to_all | solution.py:75
  63.3 3.8 %reshape.58 = bf16[576,1440]{1,0:T(8,128)(2,1)} reshape(bf16[16,36,1440]{2,1,0:T(8,128)(2,1)} %all-to-all-done.1) | data formatting | bytes 3317760 | tf_op jit(solution)/shard_map/reshape | solution.py:82
  67.1 1.2 collective-permute-start.1
  68.3 39.7 %all-to-all-done = bf16[16,36,1456]{2,1,0:T(8,128)(2,1)S(1)} async-done(((bf16[16,36,1456]{2,1,0:T(8,128)(2,1)}), bf16[16,36,1456]{2,1,0:T(8,128)(2,1)S(1)}, u32[]{:S(2)}, u32[]{:S(2)}) %all-to-all-start) | async-done | bytes 1677344 | tf_op jit(solution)/shard_map/all_to_all | solution.py:75
  108.1 1.7 reshape.56
  109.7 1.2 collective-permute-start
  111.0 1.2 select_reduce_fusion.2
  112.1 2.2 broadcast_select_fusion.4
  114.4 9.6 %fusion.5 = f32[576,1440]{1,0:T(8,128)S(1)} fusion(bf16[1,2880,1440]{1,2,0:T(8,128)(2,1)} %param.13, bf16[576,1440]{1,0:T(8,128)(2,1)S(1)} %get-tuple-element.12, bf16[576,1440]{1,0:T(8,128)(2,1)S(1)} %get-tuple-element.11), kind=kOutput, calls=%fused_computation.8 | convolution fusion | flops 4784209920 | bytes 14929920 | tf_op jit(solution)/shard_map/dot_general | solution.py:100
  124.0 9.6 %fusion.15 = f32[576,1440]{1,0:T(8,128)} fusion(bf16[1,2880,1440]{1,2,0:T(8,128)(2,1)} %param.14, bf16[576,1440]{1,0:T(8,128)(2,1)S(1)} %get-tuple-element.12, bf16[576,1440]{1,0:T(8,128)(2,1)S(1)} %get-tuple-element.11), kind=kOutput, calls=%fused_computation.24 | convolution fusion | flops 4785039360 | bytes 14929920 | tf_op jit(solution)/shard_map/dot_general | solution.py:101
  133.6 16.6 %collective-permute-done = bf16[576,1456]{1,0:T(8,128)(2,1)S(1)} collective-permute-done((bf16[576,1456]{1,0:T(8,128)(2,1)}, bf16[576,1456]{1,0:T(8,128)(2,1)S(1)}, u32[]{:S(2)}, u32[]{:S(2)}) %collective-permute-start) | collective-permute-done | bytes 1677344 | tf_op jit(solution)/shard_map/ppermute | solution.py:14
  150.3 0.2 broadcast_select_fusion.1
  150.5 12.6 %multiply_reduce_fusion = (f32[576]{0:T(1024)S(1)}, bf16[576,1440]{1,0:T(8,128)(2,1)}, bf16[576,1440]{1,0:T(8,128)(2,1)S(1)}, bf16[576,1440]{1,0:T(8,128)(2,1)S(1)}) fusion(f32[576,1440]{1,0:T(8,128)} %fusion.15, f32[576,1440]{1,0:T(8,128)S(1)} %fusion.5, f32[576]{0:T(1024)S(1)} %select_reduce_fusion.2, bf16[1,1440,2880]{2,1,0:T(8,128)(2,1)} %param.15, ...), kind=kOutput, calls=%fused_computation.18 | convolution fusion | flops 4801627648 | bytes 23228928 | tf_op jit(solution)/shard_map/dot_general | solution.py:104
  163.2 9.4 %fusion.3 = f32[576,2880]{1,0:T(8,128)S(1)} fusion(bf16[576,1440]{1,0:T(8,128)(2,1)S(1)} %get-tuple-element.9, bf16[1,2880,1440]{1,2,0:T(8,128)(2,1)} %param.13), kind=kOutput, calls=%fused_computation.6 | convolution fusion | flops 4777574400 | bytes 16588800 | tf_op jit(solution)/shard_map/dot_general | solution.py:115
  172.6 9.5 %add_convert_fusion = bf16[576,2880]{1,0:T(8,128)(2,1)S(1)} fusion(f32[576,2880]{1,0:T(8,128)S(1)} %fusion.3, bf16[576,1440]{1,0:T(8,128)(2,1)S(1)} %get-tuple-element.10, bf16[1,2880,1440]{1,2,0:T(8,128)(2,1)} %param.14), kind=kOutput, calls=%fused_computation.17 | convolution fusion | flops 4780892160 | bytes 19906560 | tf_op jit(solution)/shard_map/dot_general | solution.py:117
  182.1 1.8 broadcast_select_fusion.2
  183.9 1.2 collective-permute-start.2
  185.1 0.3 collective-permute-start.3
  185.4 38.4 %collective-permute-done.3 = f32[576]{0:T(1024)S(1)} collective-permute-done((f32[576]{0:T(1024)S(1)}, f32[576]{0:T(1024)S(1)}, u32[]{:S(2)}, u32[]{:S(2)}) %collective-permute-start.3) | collective-permute-done | bytes 2336 | tf_op jit(solution)/shard_map/ppermute | solution.py:14
  223.8 0.6 add_convert_fusion.2
  224.4 0.9 concatenate.23
  225.3 4.0 %add_convert_fusion.1 = bf16[576,1440]{1,0:T(8,128)(2,1)} fusion(bf16[576,1440]{1,0:T(8,128)(2,1)} %collective-permute-done.2, pred[]{:T(512)S(6)} %eq.74, bf16[576,2880]{1,0:T(8,128)(2,1)S(1)} %add_convert_fusion), kind=kLoop, calls=%fused_computation.20 | loop fusion | flops 4147200 | bytes 6635521 | tf_op jit(solution)/shard_map/convert_element_type | solution.py:36
  229.3 2.6 concatenate.20
  232.0 1.5 pad_maximum_fusion.4
  233.5 6.0 %all-to-all-start.2 = ((bf16[16,36,1441]{2,1,0:T(8,128)(2,1)}), bf16[16,36,1441]{2,1,0:T(8,128)(2,1)S(1)}, u32[]{:S(2)}, u32[]{:S(2)}) async-start(bf16[16,36,1441]{2,1,0:T(8,128)(2,1)} %pad_maximum_fusion.4), calls=%async_computation.2 | async-start | bytes 3932160 | tf_op jit(solution)/shard_map/all_to_all | solution.py:75
  239.5 12.6 %fusion = bf16[1,1440,2880]{2,1,0:T(8,128)(2,1)} fusion(bf16[576,1440]{1,0:T(8,128)(2,1)} %get-tuple-element.8, f32[576]{0:T(1024)S(1)} %copy-done.14, bf16[576,1440]{1,0:T(8,128)(2,1)} %copy-done.8, bf16[576,1440]{1,0:T(8,128)(2,1)} %copy-done.7), kind=kOutput, calls=%fused_computation.3 | convolution fusion | flops 4791674880 | bytes 13273344 | tf_op jit(solution)/shard_map/dot_general | solution.py:122
  252.1 9.9 %fusion.2 = bf16[1,2880,1440]{1,2,0:T(8,128)(2,1)} fusion(bf16[576,1440]{1,0:T(8,128)(2,1)S(1)} %copy-done.19, bf16[576,1440]{1,0:T(8,128)(2,1)S(1)} %copy-done.6, bf16[576,1440]{1,0:T(8,128)(2,1)S(1)} %copy-done.4), kind=kOutput, calls=%fused_computation.5 | convolution fusion | flops 4788357120 | bytes 13271040 | tf_op jit(solution)/shard_map/dot_general | solution.py:128
  262.0 10.1 %fusion.1 = bf16[1,2880,1440]{1,2,0:T(8,128)(2,1)} fusion(bf16[576,1440]{1,0:T(8,128)(2,1)S(1)} %copy-done.21, bf16[576,1440]{1,0:T(8,128)(2,1)S(1)} %copy-done.6, bf16[576,1440]{1,0:T(8,128)(2,1)S(1)} %copy-done.4), kind=kOutput, calls=%fused_computation.4 | convolution fusion | flops 4788357120 | bytes 13271040 | tf_op jit(solution)/shard_map/dot_general | solution.py:125
  272.0 11.9 %all-to-all-done.2 = bf16[16,36,1441]{2,1,0:T(8,128)(2,1)S(1)} async-done(((bf16[16,36,1441]{2,1,0:T(8,128)(2,1)}), bf16[16,36,1441]{2,1,0:T(8,128)(2,1)S(1)}, u32[]{:S(2)}, u32[]{:S(2)}) %all-to-all-start.2) | async-done | bytes 1660064 | tf_op jit(solution)/shard_map/all_to_all | solution.py:75
  283.9 1.7 reshape.59
  285.7 1.2 convert_reduce_fusion
  286.9 1.4 convolution_bitcast_fusion
  288.3 1.1 slice.49
  289.5 0.3 select_reduce_fusion
  289.8 0.7 fusion.26
  (51 shorter events, 0.4 us)
Async XLA Ops:
  0.6 3.5 %copy-start = (bf16[384,1440]{0,1:T(8,128)(2,1)S(1)}, bf16[384,1440]{0,1:T(8,128)(2,1)}, u32[]{:S(2)}) copy-start(bf16[384,1440]{0,1:T(8,128)(2,1)} %param.8) | copy-start | bytes 3317764
  0.7 1.8 copy-start.15
  2.4 0.6 copy-start.11
  3.2 0.6 copy-start.9
  6.8 6.7 %copy-start.17 = (bf16[384,1440]{0,1:T(8,128)(2,1)S(1)}, bf16[384,1440]{0,1:T(8,128)(2,1)}, u32[]{:S(2)}) copy-start(bf16[384,1440]{0,1:T(8,128)(2,1)} %param.9) | copy-start | bytes 3317764
  6.8 51.4 %all-to-all-start.1 = ((bf16[16,36,1440]{2,1,0:T(8,128)(2,1)}), bf16[16,36,1440]{2,1,0:T(8,128)(2,1)}, u32[]{:S(2)}, u32[]{:S(2)}) async-start(bf16[16,36,1440]{2,1,0:T(8,128)(2,1)} %reshape.57), calls=%async_computation.1 | async-start | bytes 3932160 | tf_op jit(solution)/shard_map/all_to_all | solution.py:75
  58.2 49.9 %all-to-all-start = ((bf16[16,36,1456]{2,1,0:T(8,128)(2,1)}), bf16[16,36,1456]{2,1,0:T(8,128)(2,1)S(1)}, u32[]{:S(2)}, u32[]{:S(2)}) async-start(bf16[16,36,1456]{2,1,0:T(8,128)(2,1)} %reshape.55), calls=%async_computation | async-start | bytes 3932160 | tf_op jit(solution)/shard_map/all_to_all | solution.py:75
  67.1 45.0 %collective-permute-start.1 = (bf16[576,1440]{1,0:T(8,128)(2,1)}, bf16[576,1440]{1,0:T(8,128)(2,1)}, u32[]{:S(2)}, u32[]{:S(2)}) collective-permute-start(bf16[576,1440]{1,0:T(8,128)(2,1)} %reshape.58), channel_id=1, source_target_pairs={{0,1},{1,0},{2,3},{3,2},{4,5},{5,4},{6,7},{7,6},{8,9},{9,8},{10,11... | collective-permute-start | bytes 4976648 | tf_op jit(solution)/shard_map/ppermute | solution.py:14
  109.7 40.5 %collective-permute-start = (bf16[576,1456]{1,0:T(8,128)(2,1)}, bf16[576,1456]{1,0:T(8,128)(2,1)S(1)}, u32[]{:S(2)}, u32[]{:S(2)}) collective-permute-start(bf16[576,1456]{1,0:T(8,128)(2,1)} %reshape.56), channel_id=1, source_target_pairs={{0,1},{1,0},{2,3},{3,2},{4,5},{5,4},{6,7},{7,6},{8,9},{9,8},{10,11... | collective-permute-start | bytes 5031944 | tf_op jit(solution)/shard_map/ppermute | solution.py:14
  112.1 38.4 %copy-start.13 = (f32[576]{0:T(1024)}, f32[576]{0:T(1024)S(1)}, u32[]{:S(2)}) copy-start(f32[576]{0:T(1024)S(1)} %select_reduce_fusion.2) | copy-start | bytes 6916
  114.4 9.6 %copy-start.3 = (bf16[576,1440]{1,0:T(8,128)(2,1)}, bf16[576,1440]{1,0:T(8,128)(2,1)S(1)}, u32[]{:S(2)}) copy-start(bf16[576,1440]{1,0:T(8,128)(2,1)S(1)} %get-tuple-element.11) | copy-start | bytes 4976644
  114.4 9.6 %copy-start.5 = (bf16[576,1440]{1,0:T(8,128)(2,1)}, bf16[576,1440]{1,0:T(8,128)(2,1)S(1)}, u32[]{:S(2)}) copy-start(bf16[576,1440]{1,0:T(8,128)(2,1)S(1)} %get-tuple-element.12) | copy-start | bytes 4976644
  124.0 26.3 %copy-start.2 = (bf16[576,1456]{1,0:T(8,128)(2,1)S(1)}, bf16[576,1456]{1,0:T(8,128)(2,1)}, u32[]{:S(2)}) copy-start(bf16[576,1456]{1,0:T(8,128)(2,1)} %reshape.56) | copy-start | bytes 5031940
  150.5 12.7 %copy-start.7 = (bf16[576,1440]{1,0:T(8,128)(2,1)}, bf16[576,1440]{1,0:T(8,128)(2,1)S(1)}, u32[]{:S(2)}) copy-start(bf16[576,1440]{1,0:T(8,128)(2,1)S(1)} %get-tuple-element.13) | copy-start | bytes 4976644
  150.5 12.7 %copy-start.8 = (bf16[576,1440]{1,0:T(8,128)(2,1)}, bf16[576,1440]{1,0:T(8,128)(2,1)S(1)}, u32[]{:S(2)}) copy-start(bf16[576,1440]{1,0:T(8,128)(2,1)S(1)} %get-tuple-element.14) | copy-start | bytes 4976644
  163.2 9.4 %copy-start.20 = (bf16[576,1440]{1,0:T(8,128)(2,1)}, bf16[576,1440]{1,0:T(8,128)(2,1)S(1)}, u32[]{:S(2)}) copy-start(bf16[576,1440]{1,0:T(8,128)(2,1)S(1)} %get-tuple-element.9) | copy-start | bytes 4976644
  163.2 9.4 %copy-start.18 = (bf16[576,1440]{1,0:T(8,128)(2,1)}, bf16[576,1440]{1,0:T(8,128)(2,1)S(1)}, u32[]{:S(2)}) copy-start(bf16[576,1440]{1,0:T(8,128)(2,1)S(1)} %get-tuple-element.10) | copy-start | bytes 4976644
  183.9 41.4 %collective-permute-start.2 = (bf16[576,1440]{1,0:T(8,128)(2,1)}, bf16[576,1440]{1,0:T(8,128)(2,1)}, u32[]{:S(2)}, u32[]{:S(2)}) collective-permute-start(bf16[576,1440]{1,0:T(8,128)(2,1)} %broadcast_select_fusion.2), channel_id=1, source_target_pairs={{0,1},{1,0},{2,3},{3,2},{4,5},{5,4},{6,7},{7,6},{8,9},{9,8},{10,11... | collective-permute-start | bytes 4976648 | tf_op jit(solution)/shard_map/ppermute | solution.py:14
  185.1 38.6 %collective-permute-start.3 = (f32[576]{0:T(1024)S(1)}, f32[576]{0:T(1024)S(1)}, u32[]{:S(2)}, u32[]{:S(2)}) collective-permute-start(f32[576]{0:T(1024)S(1)} %get-tuple-element.7), channel_id=1, source_target_pairs={{0,1},{1,0},{2,3},{3,2},{4,5},{5,4},{6,7},{7,6},{8,9},{9,8},{10,11... | collective-permute-start | bytes 6920 | tf_op jit(solution)/shard_map/ppermute | solution.py:14
  231.9 7.5 %copy-start.14 = (f32[576]{0:T(1024)S(1)}, f32[576]{0:T(1024)}, u32[]{:S(2)}) copy-start(f32[576]{0:T(1024)} %copy-done.13) | copy-start | bytes 6916
  233.5 50.5 %all-to-all-start.2 = ((bf16[16,36,1441]{2,1,0:T(8,128)(2,1)}), bf16[16,36,1441]{2,1,0:T(8,128)(2,1)S(1)}, u32[]{:S(2)}, u32[]{:S(2)}) async-start(bf16[16,36,1441]{2,1,0:T(8,128)(2,1)} %pad_maximum_fusion.4), calls=%async_computation.2 | async-start | bytes 3932160 | tf_op jit(solution)/shard_map/all_to_all | solution.py:75
  239.4 12.6 %copy-start.4 = (bf16[576,1440]{1,0:T(8,128)(2,1)S(1)}, bf16[576,1440]{1,0:T(8,128)(2,1)}, u32[]{:S(2)}) copy-start(bf16[576,1440]{1,0:T(8,128)(2,1)} %copy-done.3) | copy-start | bytes 4976644
  239.5 12.6 %copy-start.6 = (bf16[576,1440]{1,0:T(8,128)(2,1)S(1)}, bf16[576,1440]{1,0:T(8,128)(2,1)}, u32[]{:S(2)}) copy-start(bf16[576,1440]{1,0:T(8,128)(2,1)} %copy-done.5) | copy-start | bytes 4976644
  239.5 12.6 %copy-start.19 = (bf16[576,1440]{1,0:T(8,128)(2,1)S(1)}, bf16[576,1440]{1,0:T(8,128)(2,1)}, u32[]{:S(2)}) copy-start(bf16[576,1440]{1,0:T(8,128)(2,1)} %copy-done.18) | copy-start | bytes 4976644
  252.1 9.9 %copy-start.21 = (bf16[576,1440]{1,0:T(8,128)(2,1)S(1)}, bf16[576,1440]{1,0:T(8,128)(2,1)}, u32[]{:S(2)}) copy-start(bf16[576,1440]{1,0:T(8,128)(2,1)} %copy-done.20) | copy-start | bytes 4976644
  272.0 14.9 %copy-start.10 = (s32[16,384]{1,0:T(8,128)S(1)}, s32[16,384]{1,0:T(8,128)}, u32[]{:S(2)}) copy-start(s32[16,384]{1,0:T(8,128)} %copy-done.9) | copy-start | bytes 73732
  285.7 4.8 %copy-start.1 = (bf16[384,1440]{0,1:T(8,128)(2,1)S(1)}, bf16[384,1440]{0,1:T(8,128)(2,1)}, u32[]{:S(2)}) copy-start(bf16[384,1440]{0,1:T(8,128)(2,1)} %param.8) | copy-start | bytes 3317764
  286.9 2.9 copy-start.12
  286.9 2.9 copy-start.16
